TPU v7x, 256 devices: a whole 4x4x8 slice. The times are simulated.
256 devices in a mesh: dp: 4 (over x_lo, core), ctx: 64 (over x_hi, z, y).
Axes of the slice: x: 4 (x_hi: 2, x_lo: 2; x = x_hi * 2 + x_lo), y: 4, z: 8, core: 2. Of those that a mesh axis runs over, the one named last changes fastest.
Arguments:
- inputs: bfloat16 [4, 8192, 2048], P('dp', 'ctx'), may hold values from -6 to 6
- b_proj: bfloat16 [4, 8192, 64], P('dp', 'ctx'), may hold values from -0.75 to 0.75
- c_proj: bfloat16 [4, 8192, 64], P('dp', 'ctx'), may hold values from -6 to 6
- step_sizes: float32 [4, 32, 8192], P('dp', None, 'ctx'), may hold values from 0.0001 to 0.37
- a_log: float32 [32], replicated, may hold values from -8 to -1.7
- skip_gain: float32 [32], replicated, may hold values from 0.5 to 1.5
- doc_lengths: int32 [4, 16], P('dp'), may hold values from 1 to 2048, 8192 in all within a row
- grad_out: bfloat16 [4, 8192, 2048], P('dp', 'ctx'), may hold values from -6 to 6
Outputs:
- input_grads: bfloat16 [4, 8192, 2048], P('dp', 'ctx')
- b_gradient: bfloat16 [4, 8192, 64], P('dp', 'ctx')
- c_gradient: bfloat16 [4, 8192, 64], P('dp', 'ctx')
- step_grads: float32 [4, 32, 8192], P('dp', None, 'ctx')
- alog_grads: float32 [32], replicated
- skip_grads: float32 [32], replicated
Inputs may be any that keep to these rules, and one draw needn't show every extreme that they name: `doc_lengths`: each row holds the 16 document lengths of one packed sequence, in order, summing to 8192; the longest is exactly 2048.
All inputs are finite; a program needn't handle non-finite values.
Results may differ from a plain program's by a relative error of at most 0.0012.
Values sent between devices are 32-bit elements; how exact they have to be, the bound alone decides.
A program may use at most 256 MiB of HBM per device.

v0:
```python
import jax
import jax.numpy as jnp
from jax import lax
from jax.sharding import PartitionSpec as P

GROUP = 128
very_negative = -1e30
highest = lax.Precision.HIGHEST


def prefix_2(x, axis, combine, identity, reverse):
    count, index = (lax.axis_size(axis), lax.axis_index(axis))
    everything = jax.tree.map(lambda part: lax.all_gather(part, axis), x)
    start = jax.tree.map(
        lambda part, zero: jnp.broadcast_to(jnp.asarray(zero, part.dtype), part.shape), x, identity
    )

    def step(k, before):
        at = count - 1 - k if reverse else k
        reached = at > index if reverse else at < index
        new = combine(before, jax.tree.map(lambda part: part[at], everything))
        return jax.tree.map(lambda a, b: jnp.where(reached, a, b), new, before)

    return lax.fori_loop(0, count, step, start)


def segment_ids(lengths, offset, row_count):
    starts = jnp.cumsum(lengths) - lengths
    places = offset + jnp.arange(row_count, dtype=jnp.int32)
    return jnp.sum((starts[None, :] <= places[:, None]).astype(jnp.int32), axis=1) - 1


def decay_logs(deltas, rate_log):
    return deltas * (-jnp.exp(rate_log))[:, None]


def intra_group(values, bvectors, cvectors, deltas, rate_log, segment):
    cumulated = jnp.cumsum(decay_logs(deltas, rate_log), axis=1)
    spread = cumulated[:, :, None] - cumulated[:, None, :]
    places = jnp.arange(segment.shape[0])
    allowed = (places[:, None] >= places[None, :]) & (segment[:, None] == segment[None, :])
    kernel = jnp.exp(jnp.where(allowed[None], spread, very_negative))
    scores = jnp.dot(cvectors, bvectors.T, precision=highest)
    weights = kernel * scores[None] * deltas[:, None, :]
    return jnp.einsum("hts,shp->thp", weights, values, precision=highest)


def group_cross(values, bvectors, cvectors, deltas, rate_log, segment, before, incoming):
    cumulated = jnp.cumsum(decay_logs(deltas, rate_log), axis=1)
    living = (segment == before).astype(cumulated.dtype)
    carried = jnp.exp(cumulated) * living[None, :]
    readout = (
        jnp.einsum("tn,hpn->thp", cvectors, incoming, precision=highest)
        * jnp.transpose(carried)[:, :, None]
    )
    ending = (segment == segment[-1]).astype(cumulated.dtype)
    keeping = jnp.exp(cumulated[:, -1:] - cumulated) * deltas * ending[None, :]
    weighted = values * jnp.transpose(keeping)[:, :, None]
    fresh_part = jnp.einsum("shp,sn->hpn", weighted, bvectors, precision=highest)
    return (readout, carried[:, -1][:, None, None] * incoming + fresh_part)


def intra_run(values, bvectors, cvectors, deltas, rate_log, segment):
    row_count = values.shape[0]
    group_count = row_count // GROUP
    pieces = (
        values.reshape(group_count, GROUP, values.shape[1], values.shape[2]),
        bvectors.reshape(group_count, GROUP, bvectors.shape[1]),
        cvectors.reshape(group_count, GROUP, cvectors.shape[1]),
        jnp.transpose(deltas.reshape(deltas.shape[0], group_count, GROUP), (1, 0, 2)),
        segment.reshape(group_count, GROUP),
    )

    def within(pieces_now):
        return intra_group(
            pieces_now[0], pieces_now[1], pieces_now[2], pieces_now[3], rate_log, pieces_now[4]
        )

    outcome = lax.map(jax.checkpoint(within), pieces)
    return outcome.reshape(row_count, values.shape[1], values.shape[2])


def cross_run(values, bvectors, cvectors, deltas, rate_log, segment, before, incoming):
    row_count = values.shape[0]
    group_count = row_count // GROUP
    befores = jnp.concatenate([jnp.reshape(before, (1,)), segment[GROUP - 1 :: GROUP][:-1]])
    pieces = (
        values.reshape(group_count, GROUP, values.shape[1], values.shape[2]),
        bvectors.reshape(group_count, GROUP, bvectors.shape[1]),
        cvectors.reshape(group_count, GROUP, cvectors.shape[1]),
        jnp.transpose(deltas.reshape(deltas.shape[0], group_count, GROUP), (1, 0, 2)),
        segment.reshape(group_count, GROUP),
        befores,
    )

    def advance(carried_state, pieces_now):
        readout, next_state = group_cross(
            pieces_now[0],
            pieces_now[1],
            pieces_now[2],
            pieces_now[3],
            rate_log,
            pieces_now[4],
            pieces_now[5],
            carried_state,
        )
        return (next_state, readout)

    ending_state, readout = lax.scan(jax.checkpoint(advance), incoming, pieces)
    return (readout.reshape(row_count, values.shape[1], values.shape[2]), ending_state)


def combine_pairs(earlier, later):
    return (earlier[0] * later[0], later[0][:, None, None] * earlier[1] + later[1])


def per_device(inputs, b_proj, c_proj, step_sizes, a_log, skip_gain, doc_lengths, grad_out):
    row_count = inputs.shape[1]
    head_count = a_log.shape[0]
    head_width = inputs.shape[2] // head_count
    values = inputs[0].astype(jnp.float32).reshape(row_count, head_count, head_width)
    bvectors = b_proj[0].astype(jnp.float32)
    cvectors = c_proj[0].astype(jnp.float32)
    deltas = step_sizes[0]
    lengths = doc_lengths[0]
    upstream = grad_out[0].astype(jnp.float32).reshape(row_count, head_count, head_width)
    state_width = bvectors.shape[1]
    offset = lax.axis_index("ctx") * row_count
    segment = segment_ids(lengths, offset, row_count)
    before = segment_ids(lengths, offset - 1, 1)[0]

    def local_part(value_in, bvec_in, cvec_in, delta_in, rate_in, skip_in):
        return (
            intra_run(value_in, bvec_in, cvec_in, delta_in, rate_in, segment)
            + skip_in[None, :, None] * value_in
        )

    outcome, pull_local = jax.vjp(local_part, values, bvectors, cvectors, deltas, a_log, skip_gain)
    local_grads = pull_local(upstream)
    nothing = jnp.zeros((head_count, head_width, state_width), jnp.float32)
    readout, own_states = cross_run(
        values, bvectors, cvectors, deltas, a_log, segment, before, nothing
    )
    log_decay = decay_logs(deltas, a_log)
    through = jnp.exp(jnp.sum(log_decay, axis=1)) * (segment[-1] == before).astype(jnp.float32)
    carried = (
        jnp.exp(jnp.cumsum(log_decay, axis=1)) * (segment == before).astype(jnp.float32)[None, :]
    )
    pulled = jnp.einsum(
        "thp,tn->hpn", upstream * jnp.transpose(carried)[:, :, None], cvectors, precision=highest
    )
    identity_pair = (jnp.ones((head_count,), jnp.float32), nothing)
    prefix = prefix_2((through, own_states), "ctx", combine_pairs, identity_pair, False)
    suffix = prefix_2((through, pulled), "ctx", combine_pairs, identity_pair, True)
    incoming = prefix[1]

    def cross_part(value_in, bvec_in, cvec_in, delta_in, rate_in):
        return cross_run(value_in, bvec_in, cvec_in, delta_in, rate_in, segment, before, incoming)

    outflow, pull_cross = jax.vjp(cross_part, values, bvectors, cvectors, deltas, a_log)
    cross_grads = pull_cross((upstream, suffix[1]))
    rate_grad = local_grads[4] + cross_grads[4]
    totals = lax.psum((rate_grad, local_grads[5]), ("dp", "ctx"))
    value_grads = (local_grads[0] + cross_grads[0]).reshape(row_count, head_count * head_width)
    return (
        value_grads.astype(jnp.bfloat16)[None],
        (local_grads[1] + cross_grads[1]).astype(jnp.bfloat16)[None],
        (local_grads[2] + cross_grads[2]).astype(jnp.bfloat16)[None],
        (local_grads[3] + cross_grads[3])[None],
        totals[0],
        totals[1],
    )


def solution(mesh):
    in_specs = (
        P("dp", "ctx", None),
        P("dp", "ctx", None),
        P("dp", "ctx", None),
        P("dp", None, "ctx"),
        P(),
        P(),
        P("dp", None),
        P("dp", "ctx", None),
    )
    out_specs = (
        P("dp", "ctx", None),
        P("dp", "ctx", None),
        P("dp", "ctx", None),
        P("dp", None, "ctx"),
        P(),
        P(),
    )
    return jax.shard_map(
        per_device, mesh=mesh, in_specs=in_specs, out_specs=out_specs, check_vma=False
    )
```

profile of v0, /device:TPU:1, one launch (start us, length us, event | category | flops | bytes accessed | tf_op | source)
XLA Modules:
  0.0 1448.2 jit_solution(2915126778464182989)
XLA Ops:
  14.1 1.5 copy.41
  17.0 1.6 convolution_add_fusion
  18.7 1.6 fusion.42
  22.4 164.9 %all-reduce.2 = f32[2048]{0:T(1024)S(1)} all-reduce(f32[2048]{0:T(1024)S(1)} %multiply_dynamic-update-slice_fusion), channel_id=2, replica_groups=mesh['dp'=4,'ctx'=64] {'ctx'}, use_global_device_ids=true, to_apply=%add.2 | all-reduce | flops 2048 | bytes 16384
  190.3 440.9 %all-gather.6.cloned.1.call-done = f32[2048,64,64]{2,1,0:T(8,128)} async-done(((f32[32,64,64]{2,1,0:T(8,128)}), f32[2048,64,64]{2,1,0:T(8,128)}) %all-gather.6.cloned.1.call-update) | async-done | bytes 33554448 | tf_op jit(solution)/shard_map/all_gather | solution.py:13
  631.3 97.1 %while.20 = (s32[]{:T(128)}, f32[32,64,64]{2,1,0:T(8,128)S(1)}, s32[]{:T(128)}, f32[64,32]{1,0:T(8,128)S(1)}, f32[64,32,64,64]{3,2,1,0:T(8,128)}, /*index=5*/s32[]{:T(128)}, s32[]{:T(128)}) while((s32[]{:T(128)}, f32[32,64,64]{2,1,0:T(8,128)S(1)}, s32[]{:T(128)}, f32[64,32]{1,0:T(8,128)S(1)}, f32[64,32,64,64]{3,2,1,0:T(8,128)}, ...), condition=%wide.region_7.8_spmd.clone, body=%wide.region_6.7_spmd.clone.sunk | while | flops 524292 | bytes 1573353 | solution.py:24
  644.8 1.6 fusion.67
  646.5 1.5 fusion.67
  652.5 1.5 fusion.67
  654.0 1.5 fusion.67
  663.1 1.5 fusion.67
  664.6 1.5 fusion.67
  669.2 1.5 fusion.67
  673.7 1.5 fusion.67
  675.2 1.5 fusion.67
  691.8 1.8 fusion.67
  693.6 1.6 fusion.67
  696.7 1.5 fusion.67
  699.7 1.5 fusion.67
  701.3 1.5 fusion.67
  710.3 1.5 fusion.67
  711.8 1.5 fusion.67
  725.3 1.5 fusion.67
  726.9 1.5 fusion.67
  728.4 512.3 %all-gather.8.cloned.1.call-done = f32[2048,64,64]{2,1,0:T(8,128)} async-done(((f32[32,64,64]{2,1,0:T(8,128)}), f32[2048,64,64]{2,1,0:T(8,128)}) %all-gather.8.cloned.1.call-update) | async-done | bytes 33554448 | tf_op jit(solution)/shard_map/all_gather | solution.py:13
  1240.7 97.2 %while.21 = (s32[]{:T(128)}, f32[32,64,64]{2,1,0:T(8,128)S(1)}, s32[]{:T(128)}, f32[64,32]{1,0:T(8,128)S(1)}, f32[64,32,64,64]{3,2,1,0:T(8,128)}, /*index=5*/s32[]{:T(128)}, s32[]{:T(128)}, s32[]{:T(128)}, s32[]{:T(128)}) while((s32[]{:T(128)}, f32[32,64,64]{2,1,0:T(8,128)S(1)}, s32[]{:T(128)}, f32[64,32]{1,0:T(8,128)S(1)}, ...), condition=%wide.region_9.10_spmd.clone, body=%wide.region_8.9_spmd.clone.sunk | while | flops 524296 | bytes 1573415 | solution.py:24
  1243.7 1.5 fusion.68
  1245.3 1.5 fusion.68
  1246.8 1.5 fusion.68
  1251.3 1.5 fusion.68
  1252.8 1.5 fusion.68
  1258.9 1.5 fusion.68
  1260.4 1.5 fusion.68
  1265.0 1.5 fusion.68
  1266.5 1.5 fusion.68
  1268.0 1.5 fusion.68
  1272.6 1.5 fusion.68
  1274.1 1.5 fusion.68
  1275.6 1.5 fusion.68
  1280.1 1.5 fusion.68
  1338.3 6.1 fusion.8
  1344.8 3.4 fusion.2
  1351.3 2.0 multiply_reduce_fusion.4
  1354.1 2.2 fusion.6
  1357.8 2.5 fusion.14
  1361.1 1.7 fusion.16
  1363.8 75.0 %all-reduce.3 = (f32[32]{0:T(128)}, f32[32]{0:T(128)}) all-reduce(f32[32]{0:T(128)S(1)} %multiply_add_fusion, f32[32]{0:T(128)S(1)} %reduce_sum.207), channel_id=1, replica_groups=mesh['dp'=4,'ctx'=64] {'dp','ctx'}, use_global_device_ids=true, to_apply=%region_23.24 | all-reduce | flops 64 | bytes 512 | tf_op jit(solution)/shard_map/psum | solution.py:163
  1438.9 2.5 fusion.13
  (305 shorter events, 161.0 us)
Async XLA Ops:
  7.2 9.1 copy-start.6
  7.2 624.1 %all-gather.6.cloned.1.call-start = ((), (), s32[]{:S(2)}) async-start(), calls=%async_computation | async-start | bytes 68157440 | tf_op jit(solution)/shard_map/all_gather | solution.py:13
  14.1 173.3 %copy-start.2 = (bf16[1,128,2048]{1,2,0:T(8,128)(2,1)}, bf16[1,128,2048]{1,2,0:T(8,128)(2,1)S(1)}, u32[]{:S(2)}) copy-start(bf16[1,128,2048]{1,2,0:T(8,128)(2,1)S(1)} %copy.40) | copy-start | bytes 1572868
  14.1 2.9 copy-start.8
  15.6 3.0 copy-start.4
  16.9 1.7 copy-start.7
  18.6 2.4 copy-start.11
  18.6 1222.1 %all-gather.8.cloned.1.call-start = ((), (), s32[]{:S(2)}) async-start(), calls=%async_computation.1 | async-start | bytes 68157440 | tf_op jit(solution)/shard_map/all_gather | solution.py:13
  20.3 169.5 %copy-start.9 = (f32[32]{0:T(128)S(1)}, f32[32]{0:T(128)}, u32[]{:S(2)}) copy-start(f32[32]{0:T(128)} %param.17) | copy-start | bytes 388
  1240.7 97.2 %copy-start.10 = (f32[32]{0:T(128)S(1)}, f32[32]{0:T(128)}, u32[]{:S(2)}) copy-start(f32[32]{0:T(128)} %param.16) | copy-start | bytes 388
  1338.3 6.5 copy-start
  1357.8 3.3 copy-start.3
  1357.8 3.3 copy-start.5
  1361.1 77.7 %copy-start.1 = (f32[128,32,64]{0,2,1:T(8,128)S(1)}, f32[128,32,64]{0,2,1:T(8,128)}, u32[]{:S(2)}) copy-start(f32[128,32,64]{0,2,1:T(8,128)} %convert.3) | copy-start | bytes 3145732
Sparse Core Ops, SparseCore 0:
  18.7 612.5 all-gather.5
  634.8 605.8 all-gather.7
where the time goes:
time: 1450 us
  waiting for transfers between devices  953 us (66%)
  blocking collectives  240 us (17%)
  other arithmetic  203 us (14%)
  matrix products  22.6 us (2%)
  between operations  16.3 us (1%)
    all_gather x2, waiting for transfers between devices, prefix_2(): everything = jax.tree.map(lambda part: lax.all_gather(part, axis), x)  953 us
    select_n x128, other arithmetic, step(): return jax.tree.map(lambda a, b: jnp.where(reached, a, b), new, before)  188 us
    unnamed x1, blocking collectives  165 us
    psum x1, blocking collectives, per_device(): totals = lax.psum((rate_grad, local_grads[5]), ('dp', 'ctx'))  75 us
  transfers between devices with their start and end apart: 2, of which 2 were waited for; matrix products, arithmetic and copies ran while one was open for 7% of the time, Pallas kernels for 0%

commit v1 on v0

--- a/solution.py
+++ b/solution.py
@@ -160,7 +160,7 @@
     outflow, pull_cross = jax.vjp(cross_part, values, bvectors, cvectors, deltas, a_log)
     cross_grads = pull_cross((upstream, suffix[1]))
     rate_grad = local_grads[4] + cross_grads[4]
-    totals = lax.psum((rate_grad, local_grads[5]), ("dp", "ctx"))
+    totals = lax.psum(lax.psum((rate_grad, local_grads[5]), "dp"), "ctx")
     value_grads = (local_grads[0] + cross_grads[0]).reshape(row_count, head_count * head_width)
     return (
         value_grads.astype(jnp.bfloat16)[None],

time: 1450 us -> 1560 us (1.076)
  the two profiles are of different devices: /device:TPU:1 before, /device:TPU:6 now
where the time goes in v1:
time: 1560 us
  waiting for transfers between devices  925 us (59%)
  blocking collectives  379 us (24%)
  other arithmetic  204 us (13%)
  matrix products  22.6 us (1%)
  between operations  16.3 us (1%)
    all_gather x2, waiting for transfers between devices, prefix_2(): everything = jax.tree.map(lambda part: lax.all_gather(part, axis), x)  925 us
    unnamed x1, blocking collectives  191 us
    select_n x128, other arithmetic, step(): return jax.tree.map(lambda a, b: jnp.where(reached, a, b), new, before)  189 us
    psum x2, blocking collectives, per_device(): totals = lax.psum(lax.psum((rate_grad, local_grads[5]), 'dp'), 'ctx')  188 us
  transfers between devices with their start and end apart: 2, of which 2 were waited for; matrix products, arithmetic and copies ran while one was open for 6% of the time, Pallas kernels for 0%

profile of v1, /device:TPU:6, one launch (start us, length us, event | category | flops | bytes accessed | tf_op | source)
XLA Modules:
  0.0 1559.2 jit_solution(7828142103922801369)
XLA Ops:
  14.1 1.5 copy.41
  17.0 1.6 convolution_add_fusion
  18.7 1.6 fusion.42
  22.4 191.2 %all-reduce.2 = f32[2048]{0:T(1024)S(1)} all-reduce(f32[2048]{0:T(1024)S(1)} %multiply_dynamic-update-slice_fusion), channel_id=2, replica_groups=mesh['dp'=4,'ctx'=64] {'ctx'}, use_global_device_ids=true, to_apply=%add.2 | all-reduce | flops 2048 | bytes 16384
  216.7 412.6 %all-gather.6.cloned.1.call-done = f32[2048,64,64]{2,1,0:T(8,128)} async-done(((f32[32,64,64]{2,1,0:T(8,128)}), f32[2048,64,64]{2,1,0:T(8,128)}) %all-gather.6.cloned.1.call-update) | async-done | bytes 33554448 | tf_op jit(solution)/shard_map/all_gather | solution.py:13
  629.3 97.5 %while.20 = (s32[]{:T(128)}, f32[32,64,64]{2,1,0:T(8,128)S(1)}, s32[]{:T(128)}, f32[64,32]{1,0:T(8,128)S(1)}, f32[64,32,64,64]{3,2,1,0:T(8,128)}, /*index=5*/s32[]{:T(128)}, s32[]{:T(128)}) while((s32[]{:T(128)}, f32[32,64,64]{2,1,0:T(8,128)S(1)}, s32[]{:T(128)}, f32[64,32]{1,0:T(8,128)S(1)}, f32[64,32,64,64]{3,2,1,0:T(8,128)}, ...), condition=%wide.region_7.8_spmd.clone, body=%wide.region_6.7_spmd.clone.sunk | while | flops 524292 | bytes 1573353 | solution.py:24
  642.8 1.6 fusion.67
  644.4 1.6 fusion.67
  646.1 1.6 fusion.67
  650.7 1.5 fusion.67
  652.3 1.5 fusion.67
  653.8 1.5 fusion.67
  655.3 1.5 fusion.67
  661.4 1.5 fusion.67
  662.9 1.5 fusion.67
  664.4 1.5 fusion.67
  667.5 1.5 fusion.67
  670.5 1.5 fusion.67
  673.5 1.5 fusion.67
  676.5 1.5 fusion.67
  690.1 1.8 fusion.67
  691.9 1.6 fusion.67
  693.5 1.5 fusion.67
  696.6 1.5 fusion.67
  699.6 1.5 fusion.67
  708.7 1.5 fusion.67
  723.7 1.5 fusion.67
  726.8 511.9 %all-gather.8.cloned.1.call-done = f32[2048,64,64]{2,1,0:T(8,128)} async-done(((f32[32,64,64]{2,1,0:T(8,128)}), f32[2048,64,64]{2,1,0:T(8,128)}) %all-gather.8.cloned.1.call-update) | async-done | bytes 33554448 | tf_op jit(solution)/shard_map/all_gather | solution.py:13
  1238.7 97.2 %while.21 = (s32[]{:T(128)}, f32[32,64,64]{2,1,0:T(8,128)S(1)}, s32[]{:T(128)}, f32[64,32]{1,0:T(8,128)S(1)}, f32[64,32,64,64]{3,2,1,0:T(8,128)}, /*index=5*/s32[]{:T(128)}, s32[]{:T(128)}, s32[]{:T(128)}, s32[]{:T(128)}) while((s32[]{:T(128)}, f32[32,64,64]{2,1,0:T(8,128)S(1)}, s32[]{:T(128)}, f32[64,32]{1,0:T(8,128)S(1)}, ...), condition=%wide.region_9.10_spmd.clone, body=%wide.region_8.9_spmd.clone.sunk | while | flops 524296 | bytes 1573415 | solution.py:24
  1244.8 1.5 fusion.68
  1246.3 1.5 fusion.68
  1250.8 1.5 fusion.68
  1252.3 1.5 fusion.68
  1253.9 1.5 fusion.68
  1258.4 1.5 fusion.68
  1259.9 1.5 fusion.68
  1261.4 1.5 fusion.68
  1266.0 1.5 fusion.68
  1267.5 1.5 fusion.68
  1336.3 6.1 fusion.8
  1342.8 3.4 fusion.2
  1349.3 2.0 multiply_reduce_fusion.4
  1352.0 2.2 fusion.6
  1355.8 2.5 fusion.14
  1358.3 1.7 fusion.16
  1361.8 5.8 all-reduce.4
  1367.6 182.3 %all-reduce.3 = (f32[32]{0:T(128)}, f32[32]{0:T(128)}) all-reduce(f32[32]{0:T(128)S(1)} %get-tuple-element.486, f32[32]{0:T(128)S(1)} %get-tuple-element.487), channel_id=1, replica_groups=mesh['dp'=4,'ctx'=64] {'ctx'}, use_global_device_ids=true, to_apply=%region_24.25 | all-reduce | flops 64 | bytes 512 | tf_op jit(solution)/shard_map/psum | solution.py:163
  1549.9 2.5 fusion.13
  (306 shorter events, 162.5 us)
Async XLA Ops:
  7.2 9.1 copy-start.6
  7.2 622.1 %all-gather.6.cloned.1.call-start = ((), (), s32[]{:S(2)}) async-start(), calls=%async_computation | async-start | bytes 68157440 | tf_op jit(solution)/shard_map/all_gather | solution.py:13
  14.1 199.6 %copy-start.2 = (bf16[1,128,2048]{1,2,0:T(8,128)(2,1)}, bf16[1,128,2048]{1,2,0:T(8,128)(2,1)S(1)}, u32[]{:S(2)}) copy-start(bf16[1,128,2048]{1,2,0:T(8,128)(2,1)S(1)} %copy.40) | copy-start | bytes 1572868
  14.1 2.9 copy-start.8
  15.6 3.0 copy-start.4
  16.9 1.7 copy-start.7
  18.6 2.4 copy-start.11
  18.6 1220.1 %all-gather.8.cloned.1.call-start = ((), (), s32[]{:S(2)}) async-start(), calls=%async_computation.1 | async-start | bytes 68157440 | tf_op jit(solution)/shard_map/all_gather | solution.py:13
  20.3 195.8 %copy-start.9 = (f32[32]{0:T(128)S(1)}, f32[32]{0:T(128)}, u32[]{:S(2)}) copy-start(f32[32]{0:T(128)} %param.17) | copy-start | bytes 388
  1238.7 97.2 %copy-start.10 = (f32[32]{0:T(128)S(1)}, f32[32]{0:T(128)}, u32[]{:S(2)}) copy-start(f32[32]{0:T(128)} %param.16) | copy-start | bytes 388
  1336.3 6.5 copy-start
  1355.8 2.5 copy-start.3
  1355.8 2.5 copy-start.5
  1358.3 191.6 %copy-start.1 = (f32[128,32,64]{0,2,1:T(8,128)S(1)}, f32[128,32,64]{0,2,1:T(8,128)}, u32[]{:S(2)}) copy-start(f32[128,32,64]{0,2,1:T(8,128)} %convert.3) | copy-start | bytes 3145732
Sparse Core Ops, SparseCore 0:
  18.7 610.4 all-gather.5
  632.8 605.8 all-gather.7
